TPU v7x, 32 devices: a whole 2x2x4 slice. The times are simulated.
32 devices in a mesh: grp: 4 (over z), band: 8 (over y, x, core).
Axes of the slice: x: 2, y: 2, z: 4, core: 2. Of those that a mesh axis runs over, the one named last changes fastest.
Arguments:
- latent: bfloat16 [16384, 512], P(('grp', 'band')), may hold values from -6 to 6
- obs_feat: bfloat16 [4096, 512], P(('grp', 'band')), may hold values from -6 to 6
- obs_bias: bfloat16 [4096], P(('grp', 'band')), may hold values from -240 to 240
- obs_route: int32 [512, 1], P(('grp', 'band')), may hold values from 0 to 7; in each aligned block of 16 rows (0 to 15, 16 to 31, ...) at most 2 rows name the same one
- obs_tile_mask: int32 [512, 8], P(('grp', 'band')), may hold values 0 or 1
- w_query: bfloat16 [512, 512], replicated, may hold values from -0.25 to 0.25
- w_key: bfloat16 [512, 512], replicated, may hold values from -0.25 to 0.25
- w_value: bfloat16 [512, 512], replicated, may hold values from -0.25 to 0.25
- w_out: bfloat16 [512, 512], replicated, may hold values from -0.25 to 0.25
- grad_out: bfloat16 [16384, 512], P(('grp', 'band')), may hold values from -6 to 6
Outputs:
- attended: bfloat16 [16384, 512], P(('grp', 'band'))
- grad_latent: bfloat16 [16384, 512], P(('grp', 'band'))
- grad_obs: bfloat16 [4096, 512], P(('grp', 'band'))
- grad_weights: float32 [2048, 512], P('band')
Inputs may be any that keep to these rules, and one draw needn't show every extreme that they name: `obs_route`: among the 16 blocks of one device no band is named more than 2 times, a bound that some block reaches by some device in every draw.
All inputs are finite; a program needn't handle non-finite values. No bound on the sum of `obs_tile_mask` on one device may be relied on, other than what follows from the above.
Results may differ from a plain program's by a relative error of at most 0.023.
Values may be sent and summed in bfloat16 or wider, within the bound.
A program may use at most 64 MiB of HBM per device.

v0:
```python
import math
import jax
import jax.numpy as jnp
from jax import lax
from jax.sharding import PartitionSpec as P

HEADS = 16
QTILE = 64
OB = 8
SRC_BLK = 16
CAP = 2


def band_attention(query, dattn, keys, values, key_bias, visible, head_size):
    scale = 1.0 / math.sqrt(head_size)
    lat_rows = query.shape[0]
    key_rows = keys.shape[0]
    group_width = 4 * head_size

    def per_group(index):
        start = index * group_width
        query_g = lax.dynamic_slice_in_dim(query, start, group_width, 1).reshape(
            lat_rows, 4, head_size
        )
        dattn_g = lax.dynamic_slice_in_dim(dattn, start, group_width, 1).reshape(
            lat_rows, 4, head_size
        )
        keys_g = lax.dynamic_slice_in_dim(keys, start, group_width, 1).reshape(
            key_rows, 4, head_size
        )
        values_g = lax.dynamic_slice_in_dim(values, start, group_width, 1).reshape(
            key_rows, 4, head_size
        )
        scores = (
            jnp.einsum("qhd,khd->hqk", query_g, keys_g, preferred_element_type=jnp.float32) * scale
            + key_bias[None, None, :]
        )
        masked = jnp.where(visible[None], scores, -jnp.inf)
        top = jnp.maximum(jnp.max(masked, axis=-1), 0.0)
        expo = jnp.where(visible[None], jnp.exp(scores - top[..., None]), 0.0)
        total = jnp.exp(-top) + jnp.sum(expo, axis=-1)
        prob = expo / total[..., None]
        prob_b = prob.astype(jnp.bfloat16)
        attn_g = jnp.einsum("hqk,khd->qhd", prob_b, values_g, preferred_element_type=jnp.float32)
        dprob = jnp.einsum("qhd,khd->hqk", dattn_g, values_g, preferred_element_type=jnp.float32)
        delta = jnp.sum(prob * dprob, axis=-1)
        dscore = (prob * (dprob - delta[..., None])).astype(jnp.bfloat16)
        dquery_g = (
            jnp.einsum("hqk,khd->qhd", dscore, keys_g, preferred_element_type=jnp.float32) * scale
        )
        dkeys_g = (
            jnp.einsum("hqk,qhd->khd", dscore, query_g, preferred_element_type=jnp.float32) * scale
        )
        dvalues_g = jnp.einsum("hqk,qhd->khd", prob_b, dattn_g, preferred_element_type=jnp.float32)
        return (
            attn_g.reshape(lat_rows, group_width).astype(jnp.bfloat16),
            dquery_g.reshape(lat_rows, group_width).astype(jnp.bfloat16),
            dkeys_g.reshape(key_rows, group_width).astype(jnp.bfloat16),
            dvalues_g.reshape(key_rows, group_width).astype(jnp.bfloat16),
        )

    groups = query.shape[1] // group_width
    stacked = lax.map(per_group, jnp.arange(groups))

    def unstack(piece):
        return jnp.transpose(piece, (1, 0, 2)).reshape(piece.shape[1], groups * group_width)

    return tuple((unstack(piece) for piece in stacked))


def per_device(
    latent, obs_feat, obs_bias, obs_route, obs_tile_mask, w_query, w_key, w_value, w_out, grad_out
):
    band_count = lax.axis_size("band")
    group_count = lax.axis_size("grp")
    slots = band_count * CAP
    lat_rows = latent.shape[0]
    width = latent.shape[1]
    head_size = width // HEADS
    tile_count = obs_tile_mask.shape[1]
    route = obs_route[:, 0]
    order = jnp.arange(SRC_BLK)
    earlier = order[:, None] < order[None, :]
    rank = jnp.sum(((route[:, None] == route[None, :]) & earlier).astype(jnp.int32), axis=0)
    position = route * CAP + rank
    placing = (jnp.arange(slots)[:, None] == position[None, :]).astype(jnp.bfloat16)
    send_bias = jnp.dot(
        placing, obs_bias.reshape(SRC_BLK, OB), preferred_element_type=jnp.float32
    ).astype(jnp.bfloat16)
    send_mask = jnp.dot(
        placing, obs_tile_mask.astype(jnp.bfloat16), preferred_element_type=jnp.float32
    ).astype(jnp.bfloat16)
    w_pair = jnp.concatenate([w_key, w_value], axis=1)
    send_feat = jnp.dot(
        placing, obs_feat.reshape(SRC_BLK, OB * width), preferred_element_type=jnp.float32
    ).astype(jnp.bfloat16)
    recv_feat, recv_bias, recv_mask = (
        lax.all_to_all(send_feat, "band", split_axis=0, concat_axis=0, tiled=True),
        lax.all_to_all(send_bias, "band", split_axis=0, concat_axis=0, tiled=True),
        lax.all_to_all(send_mask, "band", split_axis=0, concat_axis=0, tiled=True),
    )
    recv_rows = recv_feat.reshape(slots * OB, width)
    arrived = jnp.dot(recv_rows, w_pair, preferred_element_type=jnp.float32).astype(jnp.bfloat16)
    keys = arrived[:, :width]
    values = arrived[:, width:]
    key_bias = recv_bias.reshape(slots * OB).astype(jnp.float32)
    row_tile = jnp.arange(lat_rows) // QTILE
    tile_pick = (row_tile[:, None] == jnp.arange(tile_count)[None, :]).astype(jnp.bfloat16)
    slot_seen = jnp.dot(tile_pick, recv_mask.T, preferred_element_type=jnp.float32) > 0.5
    visible = jnp.broadcast_to(slot_seen[:, :, None], (lat_rows, slots, OB)).reshape(
        lat_rows, slots * OB
    )
    query = jnp.dot(latent, w_query, preferred_element_type=jnp.float32).astype(jnp.bfloat16)
    dattn = jnp.dot(grad_out, w_out.T, preferred_element_type=jnp.float32).astype(jnp.bfloat16)
    attn, dquery, dkeys, dvalues = band_attention(
        query, dattn, keys, values, key_bias, visible, head_size
    )
    attended = jnp.dot(attn, w_out, preferred_element_type=jnp.float32).astype(jnp.bfloat16)
    grad_latent = jnp.dot(dquery, w_query.T, preferred_element_type=jnp.float32).astype(
        jnp.bfloat16
    )
    dpair_slots = jnp.concatenate([dkeys, dvalues], axis=1)
    feat_grad = jnp.dot(dpair_slots, w_pair.T, preferred_element_type=jnp.float32).astype(
        jnp.bfloat16
    )
    returned = lax.all_to_all(
        feat_grad.reshape(slots, OB * width), "band", split_axis=0, concat_axis=0, tiled=True
    )
    grad_obs = (
        jnp.dot(placing.T, returned, preferred_element_type=jnp.float32)
        .astype(jnp.bfloat16)
        .reshape(SRC_BLK * OB, width)
    )
    grad_pair = jnp.einsum("ri,rj->ij", recv_rows, dpair_slots, preferred_element_type=jnp.float32)
    grad_wq = jnp.einsum("ri,rj->ij", latent, dquery, preferred_element_type=jnp.float32)
    grad_wo = jnp.einsum("ri,rj->ij", attn, grad_out, preferred_element_type=jnp.float32)
    term = jnp.concatenate(
        [grad_wq, grad_pair[:, :width], grad_pair[:, width:], grad_wo], axis=0
    ) / float(group_count)
    band_rows = lax.psum_scatter(term.astype(jnp.bfloat16), "band", scatter_dimension=0, tiled=True)
    grads = lax.psum(band_rows, "grp").astype(jnp.float32)
    return (attended, grad_latent, grad_obs, grads)


def solution(mesh):
    return jax.shard_map(
        per_device,
        mesh=mesh,
        in_specs=(
            P(("grp", "band"), None),
            P(("grp", "band"), None),
            P(("grp", "band")),
            P(("grp", "band"), None),
            P(("grp", "band"), None),
            P(),
            P(),
            P(),
            P(),
            P(("grp", "band"), None),
        ),
        out_specs=(
            P(("grp", "band"), None),
            P(("grp", "band"), None),
            P(("grp", "band"), None),
            P("band", None),
        ),
        check_vma=False,
    )
```

profile of v0, /device:TPU:0, one launch (start us, length us, event | category | flops | bytes accessed | tf_op | source)
XLA Modules:
  0.0 164.6 jit_solution(14191782597755601926)
XLA Ops:
  7.2 0.9 convert_reduce_fusion
  8.1 0.7 multiply_add_fusion
  8.7 0.7 reshape.147
  9.7 0.7 copy.38
  10.3 5.2 %all-to-all-start.2 = ((bf16[8,2,8]{2,1,0:T(2,128)(2,1)}), bf16[8,2,8]{2,1,0:T(2,128)(2,1)S(1)}, u32[]{:S(2)}, u32[]{:S(2)}) async-start(bf16[8,2,8]{2,1,0:T(2,128)(2,1)} %bitcast.1), calls=%async_computation.2 | async-start | bytes 8192 | tf_op jit(solution)/shard_map/all_to_all | solution.py:99
  15.6 1.0 reshape.145
  16.8 1.1 constant_dynamic-update-slice_fusion.5
  17.9 0.8 convolution_convert_fusion.10
  18.7 1.1 constant_dynamic-update-slice_fusion.4
  19.8 1.2 convolution_convert_fusion.7
  21.1 1.3 convolution_convert_fusion.6
  22.3 0.7 copy.39
  23.0 4.2 %all-to-all-start.1 = ((bf16[8,2,8]{2,1,0:T(2,128)(2,1)}), bf16[8,2,8]{2,1,0:T(2,128)(2,1)S(1)}, u32[]{:S(2)}, u32[]{:S(2)}) async-start(bf16[8,2,8]{2,1,0:T(2,128)(2,1)} %bitcast.2), calls=%async_computation.1 | async-start | bytes 8192 | tf_op jit(solution)/shard_map/all_to_all | solution.py:100
  27.2 0.8 all_to_all.28
  28.1 3.8 %all-to-all-done.1 = bf16[8,2,8]{2,1,0:T(2,128)(2,1)S(1)} async-done(((bf16[8,2,8]{2,1,0:T(2,128)(2,1)}), bf16[8,2,8]{2,1,0:T(2,128)(2,1)S(1)}, u32[]{:S(2)}, u32[]{:S(2)}) %all-to-all-start.1) | async-done | bytes 288 | tf_op jit(solution)/shard_map/all_to_all | solution.py:100
  31.9 3.4 %all-to-all-start = ((bf16[8,2,4096]{2,1,0:T(2,128)(2,1)}), bf16[8,2,4096]{2,1,0:T(2,128)(2,1)S(1)}, u32[]{:S(2)}, u32[]{:S(2)}) async-start(bf16[8,2,4096]{2,1,0:T(2,128)(2,1)} %all_to_all.28), calls=%async_computation | async-start | bytes 262144 | tf_op jit(solution)/shard_map/all_to_all | solution.py:98
  35.6 5.1 %all-to-all-done = bf16[8,2,4096]{2,1,0:T(2,128)(2,1)S(1)} async-done(((bf16[8,2,4096]{2,1,0:T(2,128)(2,1)}), bf16[8,2,4096]{2,1,0:T(2,128)(2,1)S(1)}, u32[]{:S(2)}, u32[]{:S(2)}) %all-to-all-start) | async-done | bytes 131104 | tf_op jit(solution)/shard_map/all_to_all | solution.py:98
  41.1 30.6 %while.17 = (s32[]{:T(128)}, bf16[4,512,128]{1,2,0:T(8,128)(2,1)}, bf16[4,512,128]{1,2,0:T(8,128)(2,1)}, bf16[4,128,128]{1,2,0:T(8,128)(2,1)}, bf16[4,128,128]{1...) while((s32[]{:T(128)}, bf16[4,512,128]{1,2,0:T(8,128)(2,1)}, ...), condition=%wide.region_5.6_spmd.clone, body=%wide.region_1.5_spmd.clone.sunk | while | flops 107726848 | bytes 13525743 | solution.py:63
  41.2 0.6 dynamic_slice.34
  42.5 0.9 constant_dynamic-slice_fusion.9
  44.2 0.9 constant_dynamic-slice_fusion.10
  46.8 0.7 constant_dynamic-update-slice_fusion.8
  48.1 0.7 constant_dynamic-update-slice_fusion.9
  48.8 0.6 dynamic_slice.34
  50.1 0.9 constant_dynamic-slice_fusion.9
  51.8 0.9 constant_dynamic-slice_fusion.10
  54.4 0.7 constant_dynamic-update-slice_fusion.8
  55.8 0.7 constant_dynamic-update-slice_fusion.9
  57.8 0.9 constant_dynamic-slice_fusion.9
  59.5 0.9 constant_dynamic-slice_fusion.10
  62.1 0.7 constant_dynamic-update-slice_fusion.8
  63.5 0.7 constant_dynamic-update-slice_fusion.9
  64.1 0.6 dynamic_slice.34
  65.4 0.9 constant_dynamic-slice_fusion.9
  67.2 0.9 constant_dynamic-slice_fusion.10
  69.7 0.7 constant_dynamic-update-slice_fusion.8
  71.1 0.7 constant_dynamic-update-slice_fusion.9
  71.8 1.5 fusion.27
  74.0 0.8 copy-done.4
  75.5 1.9 %fusion.11 = bf16[2048,512]{1,0:T(8,128)(2,1)} fusion(f32[512,512]{1,0:T(8,128)S(1)} %fusion.27, f32[512,512]{1,0:T(8,128)S(1)} %get-tuple-element.169, f32[512,512]{1,0:T(8,128)S(1)} %get-tuple-element.168, f32[512,512]{1,0:T(8,128)S(1)} %convolution_bitcast_fusion), kind=kLoop, calls=%fused_computation.31 | loop fusion | flops 5242880 | bytes 6291456 | tf_op jit(solution)/shard_map/convert_element_type | solution.py:140
  77.9 0.7 all_to_all.35
  78.6 3.4 %all-to-all-start.3 = ((bf16[8,2,4096]{2,1,0:T(2,128)(2,1)}), bf16[8,2,4096]{2,1,0:T(2,128)(2,1)S(1)}, u32[]{:S(2)}, u32[]{:S(2)}) async-start(bf16[8,2,4096]{2,1,0:T(2,128)(2,1)} %all_to_all.35), calls=%async_computation.3 | async-start | bytes 262144 | tf_op jit(solution)/shard_map/all_to_all | solution.py:126
  82.1 2.3 %convolution_convert_fusion.5 = bf16[512,512]{1,0:T(8,128)(2,1)} fusion(bf16[512,512]{0,1:T(8,128)(2,1)} %bitcast.123, bf16[512,512]{1,0:T(8,128)(2,1)S(1)} %copy-done.7), kind=kOutput, calls=%fused_computation.34 | convolution fusion | flops 268697600 | bytes 1572864 | tf_op jit(solution)/shard_map/dot_general | solution.py:118
  84.4 33.6 %reduce-scatter.2.cloned.1.call-done = bf16[256,512]{1,0:T(8,128)(2,1)} async-done(((bf16[2048,512]{1,0:T(8,128)(2,1)}), bf16[256,512]{1,0:T(8,128)(2,1)}) %reduce-scatter.2.cloned.1.call-update) | async-done | bytes 262160 | tf_op jit(solution)/shard_map/reduce_scatter | solution.py:140
  118.1 1.3 convolution_convert_fusion.4
  119.6 0.7 reshape.152
  120.4 35.6 %all-reduce.2.cloned.1.call-done = bf16[256,512]{1,0:T(8,128)(2,1)} async-done(((bf16[256,512]{1,0:T(8,128)(2,1)}), bf16[256,512]{1,0:T(8,128)(2,1)}) %all-reduce.2.cloned.1.call-update) | async-done | bytes 262160 | tf_op jit(solution)/shard_map/psum | solution.py:141
  155.9 1.8 %convert_element_type.135 = f32[256,512]{1,0:T(8,128)} convert(bf16[256,512]{1,0:T(8,128)(2,1)} %all-reduce.2.cloned.1.call-done) | non-fusion elementwise | flops 131072 | bytes 786432 | tf_op jit(solution)/shard_map/convert_element_type | solution.py:141
  (113 shorter events, 16.7 us)
Async XLA Ops:
  7.2 13.9 %copy-start = (bf16[512,512]{1,0:T(8,128)(2,1)S(1)}, bf16[512,512]{1,0:T(8,128)(2,1)}, u32[]{:S(2)}) copy-start(bf16[512,512]{1,0:T(8,128)(2,1)} %param.21) | copy-start | bytes 1572868
  7.2 12.6 %copy-start.3 = (bf16[512,512]{1,0:T(8,128)(2,1)S(1)}, bf16[512,512]{1,0:T(8,128)(2,1)}, u32[]{:S(2)}) copy-start(bf16[512,512]{1,0:T(8,128)(2,1)} %param.12) | copy-start | bytes 1572868
  7.2 12.6 %copy-start.1 = (bf16[512,512]{1,0:T(8,128)(2,1)S(1)}, bf16[512,512]{1,0:T(8,128)(2,1)}, u32[]{:S(2)}) copy-start(bf16[512,512]{1,0:T(8,128)(2,1)} %param.17) | copy-start | bytes 1572868
  10.3 12.7 %all-to-all-start.2 = ((bf16[8,2,8]{2,1,0:T(2,128)(2,1)}), bf16[8,2,8]{2,1,0:T(2,128)(2,1)S(1)}, u32[]{:S(2)}, u32[]{:S(2)}) async-start(bf16[8,2,8]{2,1,0:T(2,128)(2,1)} %bitcast.1), calls=%async_computation.2 | async-start | bytes 8192 | tf_op jit(solution)/shard_map/all_to_all | solution.py:99
  15.6 5.5 %copy-start.6 = (bf16[512,512]{1,0:T(8,128)(2,1)S(1)}, bf16[512,512]{1,0:T(8,128)(2,1)}, u32[]{:S(2)}) copy-start(bf16[512,512]{1,0:T(8,128)(2,1)} %param.20) | copy-start | bytes 1572868
  23.0 8.9 %all-to-all-start.1 = ((bf16[8,2,8]{2,1,0:T(2,128)(2,1)}), bf16[8,2,8]{2,1,0:T(2,128)(2,1)S(1)}, u32[]{:S(2)}, u32[]{:S(2)}) async-start(bf16[8,2,8]{2,1,0:T(2,128)(2,1)} %bitcast.2), calls=%async_computation.1 | async-start | bytes 8192 | tf_op jit(solution)/shard_map/all_to_all | solution.py:100
  31.9 8.8 %all-to-all-start = ((bf16[8,2,4096]{2,1,0:T(2,128)(2,1)}), bf16[8,2,4096]{2,1,0:T(2,128)(2,1)S(1)}, u32[]{:S(2)}, u32[]{:S(2)}) async-start(bf16[8,2,4096]{2,1,0:T(2,128)(2,1)} %all_to_all.28), calls=%async_computation | async-start | bytes 262144 | tf_op jit(solution)/shard_map/all_to_all | solution.py:98
  35.3 82.8 %reduce-scatter.2.cloned.1.call-start = ((), (), s32[]{:S(2)}) async-start(), calls=%async_computation.5 | async-start | bytes 2359296 | tf_op jit(solution)/shard_map/reduce_scatter | solution.py:140
  71.8 1.5 copy-start.8
  71.8 1.5 copy-start.9
  73.8 1.0 copy-start.4
  73.8 1.2 copy-start.5
  77.4 4.7 %copy-start.7 = (bf16[512,512]{1,0:T(8,128)(2,1)S(1)}, bf16[512,512]{1,0:T(8,128)(2,1)}, u32[]{:S(2)}) copy-start(bf16[512,512]{1,0:T(8,128)(2,1)} %param.20) | copy-start | bytes 1572868
  77.4 40.7 %copy-start.2 = (bf16[512,512]{1,0:T(8,128)(2,1)S(1)}, bf16[512,512]{1,0:T(8,128)(2,1)}, u32[]{:S(2)}) copy-start(bf16[512,512]{1,0:T(8,128)(2,1)} %param.17) | copy-start | bytes 1572868
  78.6 40.7 %all-to-all-start.3 = ((bf16[8,2,4096]{2,1,0:T(2,128)(2,1)}), bf16[8,2,4096]{2,1,0:T(2,128)(2,1)S(1)}, u32[]{:S(2)}, u32[]{:S(2)}) async-start(bf16[8,2,4096]{2,1,0:T(2,128)(2,1)} %all_to_all.35), calls=%async_computation.3 | async-start | bytes 262144 | tf_op jit(solution)/shard_map/all_to_all | solution.py:126
  82.0 73.9 %all-reduce.2.cloned.1.call-start = ((), (), s32[]{:S(2)}) async-start(), calls=%async_computation.6 | async-start | bytes 524288 | tf_op jit(solution)/shard_map/psum | solution.py:141
Sparse Core Ops, SparseCore 0:
  77.5 40.4 reduce-scatter.1
  120.4 35.5 all-reduce.1
where the time goes:
time: 165 us
  waiting for transfers between devices  78.2 us (47%)
  local copies, waits for them, and re-layouts  26.2 us (16%)
  matrix products  19.5 us (12%)
  starting transfers between devices  16.2 us (10%)
  between operations  14.3 us (9%)
  other arithmetic  7.41 us (4%)
  loops' own time  2.68 us (2%)
    psum x1, waiting for transfers between devices, per_device(): grads = lax.psum(band_rows, 'grp').astype(jnp.float32)  35.6 us
    reduce_scatter x1, waiting for transfers between devices, per_device(): lax.psum_scatter(term.astype(jnp.bfloat16), 'band', scatter_dimension=0,...  33.6 us
    dynamic_update_slice x8, local copies, waits for them, and re-layouts, band_attention(): stacked = lax.map(per_group, jnp.arange(groups))  5.51 us
    all_to_all x1, starting transfers between devices, per_device(): lax.all_to_all(send_bias, 'band', split_axis=0, concat_axis=0, tiled=True)  5.2 us
    all_to_all x1, waiting for transfers between devices, per_device(): lax.all_to_all(send_feat, 'band', split_axis=0, concat_axis=0, tiled=True)  5.13 us
    all_to_all x1, starting transfers between devices, per_device(): lax.all_to_all(send_mask, 'band', split_axis=0, concat_axis=0, tiled=True)  4.19 us
    dynamic_slice x8, local copies, waits for them, and re-layouts, per_group(): lax.dynamic_slice_in_dim(query, start, group_width, 1)  4.14 us
    dynamic_slice x8, local copies, waits for them, and re-layouts, per_group(): lax.dynamic_slice_in_dim(dattn, start, group_width, 1)  4.14 us
  transfers between devices with their start and end apart: 6, of which 4 were waited for; matrix products, arithmetic and copies ran while one was open for 8% of the time, Pallas kernels for 0%

commit v1 on v0

--- a/solution.py
+++ b/solution.py
@@ -3,6 +3,7 @@
 import jax.numpy as jnp
 from jax import lax
 from jax.sharding import PartitionSpec as P
+from jax.lax import all_gather
 
 HEADS = 16
 QTILE = 64
@@ -138,7 +139,11 @@
         [grad_wq, grad_pair[:, :width], grad_pair[:, width:], grad_wo], axis=0
     ) / float(group_count)
     band_rows = lax.psum_scatter(term.astype(jnp.bfloat16), "band", scatter_dimension=0, tiled=True)
-    grads = lax.psum(band_rows, "grp").astype(jnp.float32)
+
+    def values_begin(x_in, group_axis="grp"):
+        return all_gather(x_in, axis_name=group_axis).sum(axis=0)
+
+    grads = values_begin(band_rows).astype(jnp.float32)
     return (attended, grad_latent, grad_obs, grads)
 
 

time: 165 us -> 158 us (0.958)
  waiting for transfers between devices: 78.2 us -> 69.9 us
    psum x1 -> x0, waiting for transfers between devices: 35.6 us -> none  [per_device(): grads = lax.psum(band_rows, 'grp').astype(jnp.float32)]
    all_gather x0 -> x1, waiting for transfers between devices: none -> 18.5 us  [values_begin(): return all_gather(x_in, axis_name=group_axis).sum(axis=0)]
    reduce_scatter x1, waiting for transfers between devices: 33.6 us -> 40.6 us  [per_device(): lax.psum_scatter(term.astype(jnp.bfloat16), 'band', scatter_dimension=0,...]
    all_to_all x1, waiting for transfers between devices: 0.01 us -> 1.84 us  [per_device(): lax.all_to_all(feat_grad.reshape(slots, OB * width), 'band', split_axis=0...]
  transfers between devices with their start and end apart: 6 -> 6, of which waited for: 4 -> 5; matrix products, arithmetic and copies ran while one was open for 8% -> 8% of each run, Pallas kernels for 0% -> 0%
where the time goes in v1:
time: 158 us; the launch traced here: 157 us
  waiting for transfers between devices  69.9 us (44%)
  local copies, waits for them, and re-layouts  26.2 us (17%)
  matrix products  19.5 us (12%)
  starting transfers between devices  16.2 us (10%)
  between operations  14.3 us (9%)
  other arithmetic  7.92 us (5%)
  loops' own time  2.68 us (2%)
    reduce_scatter x1, waiting for transfers between devices, per_device(): lax.psum_scatter(term.astype(jnp.bfloat16), 'band', scatter_dimension=0,...  40.6 us
    all_gather x1, waiting for transfers between devices, values_begin(): return all_gather(x_in, axis_name=group_axis).sum(axis=0)  18.5 us
    dynamic_update_slice x8, local copies, waits for them, and re-layouts, band_attention(): stacked = lax.map(per_group, jnp.arange(groups))  5.51 us
    all_to_all x1, starting transfers between devices, per_device(): lax.all_to_all(send_bias, 'band', split_axis=0, concat_axis=0, tiled=True)  5.2 us
    all_to_all x1, waiting for transfers between devices, per_device(): lax.all_to_all(send_feat, 'band', split_axis=0, concat_axis=0, tiled=True)  5.13 us
    all_to_all x1, starting transfers between devices, per_device(): lax.all_to_all(send_mask, 'band', split_axis=0, concat_axis=0, tiled=True)  4.19 us
    dynamic_slice x8, local copies, waits for them, and re-layouts, per_group(): lax.dynamic_slice_in_dim(query, start, group_width, 1)  4.14 us
    dynamic_slice x8, local copies, waits for them, and re-layouts, per_group(): lax.dynamic_slice_in_dim(dattn, start, group_width, 1)  4.14 us
  transfers between devices with their start and end apart: 6, of which 5 were waited for; matrix products, arithmetic and copies ran while one was open for 8% of the time, Pallas kernels for 0%

profile of v1, /device:TPU:0, one launch (start us, length us, event | category | flops | bytes accessed | tf_op | source)
XLA Modules:
  0.0 156.8 jit_solution(9885838697826232023)
XLA Ops:
  7.2 0.9 convert_reduce_fusion
  8.1 0.7 multiply_add_fusion
  8.7 0.7 reshape.147
  9.7 0.7 copy.38
  10.3 5.2 %all-to-all-start.2 = ((bf16[8,2,8]{2,1,0:T(2,128)(2,1)}), bf16[8,2,8]{2,1,0:T(2,128)(2,1)S(1)}, u32[]{:S(2)}, u32[]{:S(2)}) async-start(bf16[8,2,8]{2,1,0:T(2,128)(2,1)} %bitcast.1), calls=%async_computation.2 | async-start | bytes 8192 | tf_op jit(solution)/shard_map/all_to_all | solution.py:100
  15.6 1.0 reshape.145
  16.8 1.1 constant_dynamic-update-slice_fusion.5
  17.9 0.8 convolution_convert_fusion.10
  18.7 1.1 constant_dynamic-update-slice_fusion.4
  19.8 1.2 convolution_convert_fusion.7
  21.1 1.3 convolution_convert_fusion.6
  22.3 0.7 copy.39
  23.0 4.2 %all-to-all-start.1 = ((bf16[8,2,8]{2,1,0:T(2,128)(2,1)}), bf16[8,2,8]{2,1,0:T(2,128)(2,1)S(1)}, u32[]{:S(2)}, u32[]{:S(2)}) async-start(bf16[8,2,8]{2,1,0:T(2,128)(2,1)} %bitcast.2), calls=%async_computation.1 | async-start | bytes 8192 | tf_op jit(solution)/shard_map/all_to_all | solution.py:101
  27.2 0.8 all_to_all.28
  28.1 3.8 %all-to-all-done.1 = bf16[8,2,8]{2,1,0:T(2,128)(2,1)S(1)} async-done(((bf16[8,2,8]{2,1,0:T(2,128)(2,1)}), bf16[8,2,8]{2,1,0:T(2,128)(2,1)S(1)}, u32[]{:S(2)}, u32[]{:S(2)}) %all-to-all-start.1) | async-done | bytes 288 | tf_op jit(solution)/shard_map/all_to_all | solution.py:101
  31.9 3.4 %all-to-all-start = ((bf16[8,2,4096]{2,1,0:T(2,128)(2,1)}), bf16[8,2,4096]{2,1,0:T(2,128)(2,1)S(1)}, u32[]{:S(2)}, u32[]{:S(2)}) async-start(bf16[8,2,4096]{2,1,0:T(2,128)(2,1)} %all_to_all.28), calls=%async_computation | async-start | bytes 262144 | tf_op jit(solution)/shard_map/all_to_all | solution.py:99
  35.6 5.1 %all-to-all-done = bf16[8,2,4096]{2,1,0:T(2,128)(2,1)S(1)} async-done(((bf16[8,2,4096]{2,1,0:T(2,128)(2,1)}), bf16[8,2,4096]{2,1,0:T(2,128)(2,1)S(1)}, u32[]{:S(2)}, u32[]{:S(2)}) %all-to-all-start) | async-done | bytes 131104 | tf_op jit(solution)/shard_map/all_to_all | solution.py:99
  41.1 30.6 %while.17 = (s32[]{:T(128)}, bf16[4,512,128]{1,2,0:T(8,128)(2,1)}, bf16[4,512,128]{1,2,0:T(8,128)(2,1)}, bf16[4,128,128]{1,2,0:T(8,128)(2,1)}, bf16[4,128,128]{1...) while((s32[]{:T(128)}, bf16[4,512,128]{1,2,0:T(8,128)(2,1)}, ...), condition=%wide.region_5.6_spmd.clone, body=%wide.region_1.5_spmd.clone.sunk | while | flops 107726848 | bytes 13525743 | solution.py:64
  41.2 0.6 dynamic_slice.34
  42.5 0.9 constant_dynamic-slice_fusion.9
  44.2 0.9 constant_dynamic-slice_fusion.10
  46.8 0.7 constant_dynamic-update-slice_fusion.8
  48.1 0.7 constant_dynamic-update-slice_fusion.9
  50.1 0.9 constant_dynamic-slice_fusion.9
  51.8 0.9 constant_dynamic-slice_fusion.10
  54.4 0.7 constant_dynamic-update-slice_fusion.8
  55.8 0.7 constant_dynamic-update-slice_fusion.9
  57.8 0.9 constant_dynamic-slice_fusion.9
  59.5 0.9 constant_dynamic-slice_fusion.10
  62.1 0.7 constant_dynamic-update-slice_fusion.8
  63.5 0.7 constant_dynamic-update-slice_fusion.9
  65.4 0.9 constant_dynamic-slice_fusion.9
  67.2 0.9 constant_dynamic-slice_fusion.10
  69.7 0.7 constant_dynamic-update-slice_fusion.8
  71.1 0.7 constant_dynamic-update-slice_fusion.9
  71.8 1.5 fusion.27
  74.0 0.8 copy-done.4
  75.5 1.9 %fusion.11 = bf16[2048,512]{1,0:T(8,128)(2,1)} fusion(f32[512,512]{1,0:T(8,128)S(1)} %fusion.27, f32[512,512]{1,0:T(8,128)S(1)} %get-tuple-element.169, f32[512,512]{1,0:T(8,128)S(1)} %get-tuple-element.168, f32[512,512]{1,0:T(8,128)S(1)} %convolution_bitcast_fusion), kind=kLoop, calls=%fused_computation.31 | loop fusion | flops 5242880 | bytes 6291456 | tf_op jit(solution)/shard_map/convert_element_type | solution.py:141
  77.5 40.6 %reduce-scatter.2.cloned.1.call-done = bf16[256,512]{1,0:T(8,128)(2,1)} async-done(((bf16[2048,512]{1,0:T(8,128)(2,1)}), bf16[256,512]{1,0:T(8,128)(2,1)}) %reduce-scatter.2.cloned.1.call-update) | async-done | bytes 262160 | tf_op jit(solution)/shard_map/reduce_scatter | solution.py:141
  118.5 0.7 all_to_all.35
  119.3 3.4 %all-to-all-start.3 = ((bf16[8,2,4096]{2,1,0:T(2,128)(2,1)}), bf16[8,2,4096]{2,1,0:T(2,128)(2,1)S(1)}, u32[]{:S(2)}, u32[]{:S(2)}) async-start(bf16[8,2,4096]{2,1,0:T(2,128)(2,1)} %all_to_all.35), calls=%async_computation.3 | async-start | bytes 262144 | tf_op jit(solution)/shard_map/all_to_all | solution.py:127
  122.7 2.3 %convolution_convert_fusion.5 = bf16[512,512]{1,0:T(8,128)(2,1)} fusion(bf16[512,512]{0,1:T(8,128)(2,1)} %bitcast.125, bf16[512,512]{1,0:T(8,128)(2,1)S(1)} %copy-done.7), kind=kOutput, calls=%fused_computation.34 | convolution fusion | flops 268697600 | bytes 1572864 | tf_op jit(solution)/shard_map/dot_general | solution.py:119
  125.0 1.3 convolution_convert_fusion.4
  126.3 1.8 %all-to-all-done.3 = bf16[8,2,4096]{2,1,0:T(2,128)(2,1)S(1)} async-done(((bf16[8,2,4096]{2,1,0:T(2,128)(2,1)}), bf16[8,2,4096]{2,1,0:T(2,128)(2,1)S(1)}, u32[]{:S(2)}, u32[]{:S(2)}) %all-to-all-start.3) | async-done | bytes 131104 | tf_op jit(solution)/shard_map/all_to_all | solution.py:127
  128.4 0.7 reshape.152
  129.1 18.5 %all-gather.3.cloned.1.call-done = bf16[1024,512]{1,0:T(8,128)(2,1)} async-done(((bf16[256,512]{1,0:T(8,128)(2,1)}), bf16[1024,512]{1,0:T(8,128)(2,1)}) %all-gather.3.cloned.1.call-update) | async-done | bytes 1048592 | tf_op jit(solution)/shard_map/all_gather | solution.py:144
  147.6 1.5 reduce_sum.40
  149.1 0.9 convert_element_type.137
  (114 shorter events, 17.8 us)
Async XLA Ops:
  7.2 13.9 %copy-start = (bf16[512,512]{1,0:T(8,128)(2,1)S(1)}, bf16[512,512]{1,0:T(8,128)(2,1)}, u32[]{:S(2)}) copy-start(bf16[512,512]{1,0:T(8,128)(2,1)} %param.21) | copy-start | bytes 1572868
  7.2 12.6 %copy-start.3 = (bf16[512,512]{1,0:T(8,128)(2,1)S(1)}, bf16[512,512]{1,0:T(8,128)(2,1)}, u32[]{:S(2)}) copy-start(bf16[512,512]{1,0:T(8,128)(2,1)} %param.12) | copy-start | bytes 1572868
  7.2 12.6 %copy-start.1 = (bf16[512,512]{1,0:T(8,128)(2,1)S(1)}, bf16[512,512]{1,0:T(8,128)(2,1)}, u32[]{:S(2)}) copy-start(bf16[512,512]{1,0:T(8,128)(2,1)} %param.17) | copy-start | bytes 1572868
  10.3 12.7 %all-to-all-start.2 = ((bf16[8,2,8]{2,1,0:T(2,128)(2,1)}), bf16[8,2,8]{2,1,0:T(2,128)(2,1)S(1)}, u32[]{:S(2)}, u32[]{:S(2)}) async-start(bf16[8,2,8]{2,1,0:T(2,128)(2,1)} %bitcast.1), calls=%async_computation.2 | async-start | bytes 8192 | tf_op jit(solution)/shard_map/all_to_all | solution.py:100
  15.6 5.5 %copy-start.6 = (bf16[512,512]{1,0:T(8,128)(2,1)S(1)}, bf16[512,512]{1,0:T(8,128)(2,1)}, u32[]{:S(2)}) copy-start(bf16[512,512]{1,0:T(8,128)(2,1)} %param.20) | copy-start | bytes 1572868
  23.0 8.9 %all-to-all-start.1 = ((bf16[8,2,8]{2,1,0:T(2,128)(2,1)}), bf16[8,2,8]{2,1,0:T(2,128)(2,1)S(1)}, u32[]{:S(2)}, u32[]{:S(2)}) async-start(bf16[8,2,8]{2,1,0:T(2,128)(2,1)} %bitcast.2), calls=%async_computation.1 | async-start | bytes 8192 | tf_op jit(solution)/shard_map/all_to_all | solution.py:101
  31.9 8.8 %all-to-all-start = ((bf16[8,2,4096]{2,1,0:T(2,128)(2,1)}), bf16[8,2,4096]{2,1,0:T(2,128)(2,1)S(1)}, u32[]{:S(2)}, u32[]{:S(2)}) async-start(bf16[8,2,4096]{2,1,0:T(2,128)(2,1)} %all_to_all.28), calls=%async_computation | async-start | bytes 262144 | tf_op jit(solution)/shard_map/all_to_all | solution.py:99
  35.3 82.8 %reduce-scatter.2.cloned.1.call-start = ((), (), s32[]{:S(2)}) async-start(), calls=%async_computation.5 | async-start | bytes 2359296 | tf_op jit(solution)/shard_map/reduce_scatter | solution.py:141
  71.8 1.5 copy-start.8
  71.8 1.5 copy-start.9
  73.8 1.0 copy-start.4
  73.8 1.2 copy-start.5
  77.4 45.3 %copy-start.7 = (bf16[512,512]{1,0:T(8,128)(2,1)S(1)}, bf16[512,512]{1,0:T(8,128)(2,1)}, u32[]{:S(2)}) copy-start(bf16[512,512]{1,0:T(8,128)(2,1)} %param.20) | copy-start | bytes 1572868
  77.4 47.6 %copy-start.2 = (bf16[512,512]{1,0:T(8,128)(2,1)S(1)}, bf16[512,512]{1,0:T(8,128)(2,1)}, u32[]{:S(2)}) copy-start(bf16[512,512]{1,0:T(8,128)(2,1)} %param.17) | copy-start | bytes 1572868
  77.4 70.2 %all-gather.3.cloned.1.call-start = ((), (), s32[]{:S(2)}) async-start(), calls=%async_computation.6 | async-start | bytes 1310720 | tf_op jit(solution)/shard_map/all_gather | solution.py:144
  119.3 8.8 %all-to-all-start.3 = ((bf16[8,2,4096]{2,1,0:T(2,128)(2,1)}), bf16[8,2,4096]{2,1,0:T(2,128)(2,1)S(1)}, u32[]{:S(2)}, u32[]{:S(2)}) async-start(bf16[8,2,4096]{2,1,0:T(2,128)(2,1)} %all_to_all.35), calls=%async_computation.3 | async-start | bytes 262144 | tf_op jit(solution)/shard_map/all_to_all | solution.py:127
Sparse Core Ops, SparseCore 0:
  77.5 40.4 reduce-scatter.1
  119.6 27.9 all-gather.2
